TPU v7x, 512 devices: a whole 4x4x16 slice. The times are simulated.
512 devices in a mesh: dom: 64 (over y, z_hi, x, core), feat: 8 (over z_lo).
Axes of the slice: x: 4, y: 4, z: 16 (z_hi: 2, z_lo: 8; z = z_hi * 8 + z_lo), core: 2. Of those that a mesh axis runs over, the one named last changes fastest.
Arguments:
- features: bfloat16 [32768, 1024], P('dom', 'feat'), may hold values from -16 to 16
- weights: bfloat16 [2048, 1024], P(None, 'feat'), may hold values from -4 to 4
- send_rows: int32 [64, 64, 128], P('dom'), may hold values from -1 to 511, as said below
- remote_src: int32 [64, 64], P('dom'), may hold values from 0 to 63, each once within a row
- local_adj: bfloat16 [32768, 512], P('dom')
- remote_adj: bfloat16 [32768, 16, 128], P('dom')
- degree: int32 [32768], P('dom'), may hold values from 48 to 143
- cotangent: bfloat16 [32768, 1024], P('dom', 'feat'), may hold values from -6 to 6
Outputs:
- output: bfloat16 [32768, 1024], P('dom', 'feat')
- grad_input: bfloat16 [32768, 1024], P('dom', 'feat')
- grad_weights: float32 [2048, 1024], P('dom', 'feat')
Inputs may be any that keep to these rules, and one draw needn't show every extreme that they name: `send_rows`: each entry is a row of partition p or -1; in each block the used places come first and name distinct rows; a quarter or more of each block is used, and some block is full. `remote_src`: each row names every partition once.
All inputs are finite; a program needn't handle non-finite values.
Results may differ from a plain program's by a relative error of at most 0.01.
Values may be sent and summed in bfloat16 or wider, within the bound.
A program may use at most 64 MiB of HBM per device.

v0:
```python
import math
import jax
import jax.numpy as jnp
from jax import lax
from jax.sharding import PartitionSpec as P


def per_device(features, weights, send_rows, remote_src, local_adj, remote_adj, degree, cotangent):
    np_rows, feat_width = features.shape
    feat_count = lax.axis_size("feat")
    dom_count = lax.axis_size("dom")
    full_width = feat_width * feat_count
    tile_rows = remote_adj.shape[2]
    block_count = np_rows // tile_rows
    remote_span = remote_adj.shape[1] * tile_rows
    rows_out = send_rows[0]
    live_mask = rows_out >= 0
    safe_rows = jnp.where(live_mask, rows_out, 0)
    outgoing = jnp.where(live_mask[:, :, None], features[safe_rows], jnp.zeros((), jnp.bfloat16))
    halo_rows = lax.all_to_all(outgoing, "dom", split_axis=0, concat_axis=0, tiled=True)
    slot_order = remote_src[0]
    ordered = jnp.take(halo_rows, slot_order, axis=0).reshape(block_count, remote_span, feat_width)
    remote_tiles = remote_adj.reshape(block_count, tile_rows, remote_span)
    remote_sums = jnp.einsum(
        "bik,bkf->bif", remote_tiles, ordered, preferred_element_type=jnp.float32
    ).reshape(np_rows, feat_width)
    local_sums = jnp.dot(local_adj, features, preferred_element_type=jnp.float32)
    degree_col = degree.astype(jnp.float32)[:, None]
    aggregate = ((local_sums + remote_sums) / degree_col).astype(jnp.bfloat16)
    stacked = jnp.stack([features, aggregate], axis=1)
    weight_pair = weights.reshape(2, full_width, feat_width)
    gathered = lax.all_gather(stacked, "feat", axis=2, tiled=True)
    preact = jnp.einsum("rkc,kcf->rf", gathered, weight_pair, preferred_element_type=jnp.float32)
    output = jax.nn.silu(preact).astype(jnp.bfloat16)
    sigmoid_z = jax.nn.sigmoid(preact)
    grad_pre = (
        cotangent.astype(jnp.float32) * sigmoid_z * (1.0 + preact * (1.0 - sigmoid_z))
    ).astype(jnp.bfloat16)
    scaled_grad = (grad_pre.astype(jnp.float32) / degree_col).astype(jnp.bfloat16)
    back_ordered = jnp.einsum(
        "bik,bif->bkf",
        remote_tiles,
        scaled_grad.reshape(block_count, tile_rows, feat_width),
        preferred_element_type=jnp.float32,
    )
    back_ordered = back_ordered.reshape(slot_order.shape[0], tile_rows, feat_width).astype(
        jnp.bfloat16
    )
    returning = jnp.zeros_like(back_ordered).at[slot_order].set(back_ordered)
    arriving = lax.all_to_all(returning, "dom", split_axis=0, concat_axis=0, tiled=True)
    target_rows = jnp.where(live_mask, rows_out, np_rows).reshape(-1)
    neigh_grad = lax.dot_general(
        local_adj, scaled_grad, (((0,), (0,)), ((), ())), preferred_element_type=jnp.float32
    )
    neigh_grad = neigh_grad.at[target_rows].add(
        arriving.reshape(-1, feat_width).astype(jnp.float32), mode="drop"
    )
    neigh_grad = neigh_grad.astype(jnp.bfloat16)
    back_pair = jnp.stack([grad_pre, neigh_grad], axis=1)
    partial_terms = jnp.einsum(
        "rkf,kcf->rc", back_pair, weight_pair, preferred_element_type=jnp.float32
    )
    grad_input = lax.psum_scatter(partial_terms, "feat", scatter_dimension=1, tiled=True).astype(
        jnp.bfloat16
    )
    weight_scale = 1.0 / math.sqrt(dom_count * np_rows)
    combined = gathered.reshape(np_rows, 2 * full_width)
    summed = lax.psum_scatter(
        lax.dot_general(
            combined, grad_pre, (((0,), (0,)), ((), ())), preferred_element_type=jnp.float32
        ),
        "dom",
        scatter_dimension=0,
        tiled=True,
    )
    grad_weights = summed * weight_scale
    return (output, grad_input, grad_weights)


def solution(mesh):
    in_specs = (
        P("dom", "feat"),
        P(None, "feat"),
        P("dom", None, None),
        P("dom", None),
        P("dom", None),
        P("dom", None, None),
        P("dom"),
        P("dom", "feat"),
    )
    out_specs = (P("dom", "feat"), P("dom", "feat"), P("dom", "feat"))
    return jax.shard_map(
        per_device, mesh=mesh, in_specs=in_specs, out_specs=out_specs, check_vma=False
    )
```

profile of v0, /device:TPU:8, one launch (start us, length us, event | category | flops | bytes accessed | tf_op | source)
XLA Modules:
  0.0 959.6 jit_solution(17300601197789234725)
XLA Ops:
  7.2 0.0 copy-start
  7.2 0.8 compare_bitcast_fusion
  8.0 0.8 fusion.10
  8.8 22.8 %gather_fusion = bf16[8192,128]{1,0:T(8,128)(2,1)S(1)} fusion(bf16[512,128]{1,0:T(8,128)(2,1)} %param.8, s32[8192]{0:T(1024)S(1)} %fusion.10), kind=kCustom, calls=%fused_computation | custom fusion | bytes 4227072 | tf_op jit(solution)/shard_map/gather | solution.py:19
  31.6 2.6 broadcast_select_fusion
  34.2 0.0 copy-start.6
  34.2 0.0 copy-start.4
  34.2 21.5 %all-to-all-start = ((bf16[64,128,128]{2,1,0:T(8,128)(2,1)}), bf16[64,128,128]{2,1,0:T(8,128)(2,1)}, u32[]{:S(2)}, u32[]{:S(2)}) async-start(bf16[64,128,128]{2,1,0:T(8,128)(2,1)} %broadcast_select_fusion), calls=%async_computation | async-start | bytes 4194304 | tf_op jit(solution)/shard_map/all_to_all | solution.py:20
  55.7 0.0 all-gather.2.cloned.1.call-start
  55.8 0.5 broadcast.123
  56.3 0.0 copy-done.6
  56.3 0.7 reduce.3
  57.0 0.1 squeeze.10
  57.1 0.0 copy-done.4
  57.1 0.1 broadcast_bitcast_fusion
  57.2 2.8 reshape.130
  60.0 47.1 %all-to-all-done = bf16[64,128,128]{2,1,0:T(8,128)(2,1)} async-done(((bf16[64,128,128]{2,1,0:T(8,128)(2,1)}), bf16[64,128,128]{2,1,0:T(8,128)(2,1)}, u32[]{:S(2)}, u32[]{:S(2)}) %all-to-all-start) | async-done | bytes 2097184 | tf_op jit(solution)/shard_map/all_to_all | solution.py:20
  107.1 3.7 gather_fusion.1
  110.8 4.4 bitcast_select_fusion
  115.2 0.0 copy-start.1
  115.2 0.0 copy-start.2
  115.2 0.7 fusion.14
  115.9 0.0 copy-start.5
  115.9 0.1 copy-done.1
  116.1 0.2 copy-done.2
  116.3 0.3 fusion.5
  116.6 0.7 pad_maximum_fusion
  117.3 0.0 all-gather.2.cloned.1.call-update
  117.3 116.5 %all-gather.2.cloned.1.call-done = bf16[512,2,1024]{2,0,1:T(8,128)(2,1)} async-done(((bf16[512,2,128]{2,0,1:T(8,128)(2,1)}), bf16[512,2,1024]{2,0,1:T(8,128)(2,1)}) %all-gather.2.cloned.1.call-update) | async-done | bytes 2097168 | tf_op jit(solution)/shard_map/all_gather | solution.py:32
  233.8 0.0 copy-done
  233.8 0.0 copy-done.5
  233.8 3.0 divide_convert_fusion
  236.8 2.1 fusion.2
  238.9 3.0 copy.14
  241.9 1.8 broadcast_in_dim.39
  243.7 8.6 scatter_fusion
  252.4 9.3 all-to-all-start.1
  261.6 0.0 reduce-scatter.5.cloned.1.call-start
  261.7 3.9 copy.16
  265.6 0.0 copy-start.3
  265.6 3.3 fusion.13
  268.9 0.0 reduce-scatter.5.cloned.1.call-update
  268.9 0.0 reduce-scatter.3.cloned.1.call-start
  269.0 0.0 copy-done.3
  269.0 0.1 compare_select_fusion
  269.0 1.3 convolution_bitcast_fusion.1
  270.3 0.1 copy.15
  270.5 33.9 %all-to-all-done.1 = bf16[64,128,128]{2,1,0:T(8,128)(2,1)S(1)} async-done(((bf16[64,128,128]{2,1,0:T(8,128)(2,1)}), bf16[64,128,128]{2,1,0:T(8,128)(2,1)S(1)}, u32[]{:S(2)}, u32[]{:S(2)}) %all-to-all-start.1) | async-done | bytes 2097184 | tf_op jit(solution)/shard_map/all_to_all | solution.py:50
  304.4 44.3 %scatter_custom_fusion.1 = f32[512,128]{1,0:T(8,128)S(1)} fusion(f32[512,128]{1,0:T(8,128)S(1)} %copy.15, s32[8192]{0:T(1024)S(1)} %bitcast.73, bf16[8192,128]{1,0:T(8,128)(2,1)S(1)} %bitcast.65), kind=kCustom, calls=%fused_computation.4 | custom fusion | flops 2097152 | bytes 2359296 | tf_op jit(solution)/shard_map/scatter-add | solution.py:55
  348.7 1.8 convolution_bitcast_fusion
  350.5 0.0 reduce-scatter.3.cloned.1.call-update
  350.6 499.3 %reduce-scatter.5.cloned.1.call-done = f32[32,128]{1,0:T(8,128)} async-done(((f32[2048,128]{1,0:T(8,128)}), f32[32,128]{1,0:T(8,128)}) %reduce-scatter.5.cloned.1.call-update) | async-done | bytes 16400 | tf_op jit(solution)/shard_map/reduce_scatter | solution.py:68
  849.8 1.3 broadcast_multiply_fusion
  851.1 100.3 %reduce-scatter.3.cloned.1.call-done = f32[512,128]{1,0:T(8,128)} async-done(((f32[512,1024]{1,0:T(8,128)}), f32[512,128]{1,0:T(8,128)}) %reduce-scatter.3.cloned.1.call-update) | async-done | bytes 262160 | tf_op jit(solution)/shard_map/reduce_scatter | solution.py:63
  951.5 1.6 convert_element_type.55
  (6 shorter events, 0.0 us)
Async XLA Ops:
  7.2 226.7 %copy-start = (bf16[2048,128]{1,0:T(8,128)(2,1)S(1)}, bf16[2048,128]{1,0:T(8,128)(2,1)}, u32[]{:S(2)}) copy-start(bf16[2048,128]{1,0:T(8,128)(2,1)} %param.9) | copy-start | bytes 1572868
  34.2 22.1 %copy-start.6 = (s32[1,64]{1,0:T(1,128)S(1)}, s32[1,64]{1,0:T(1,128)}, u32[]{:S(2)}) copy-start(s32[1,64]{1,0:T(1,128)} %param.11) | copy-start | bytes 772
  34.2 22.8 %copy-start.4 = (s32[512]{0:T(512)S(1)}, s32[512]{0:T(512)}, u32[]{:S(2)}) copy-start(s32[512]{0:T(512)} %param.14) | copy-start | bytes 6148
  34.2 72.9 %all-to-all-start = ((bf16[64,128,128]{2,1,0:T(8,128)(2,1)}), bf16[64,128,128]{2,1,0:T(8,128)(2,1)}, u32[]{:S(2)}, u32[]{:S(2)}) async-start(bf16[64,128,128]{2,1,0:T(8,128)(2,1)} %broadcast_select_fusion), calls=%async_computation | async-start | bytes 4194304 | tf_op jit(solution)/shard_map/all_to_all | solution.py:20
  55.7 178.1 %all-gather.2.cloned.1.call-start = ((), (), s32[]{:S(2)}) async-start(), calls=%async_computation.4 | async-start | bytes 2359296 | tf_op jit(solution)/shard_map/all_gather | solution.py:32
  115.2 0.9 copy-start.1
  115.2 1.1 copy-start.2
  115.9 117.9 %copy-start.5 = (bf16[512,128]{1,0:T(8,128)(2,1)S(1)}, bf16[512,128]{1,0:T(8,128)(2,1)}, u32[]{:S(2)}) copy-start(bf16[512,128]{1,0:T(8,128)(2,1)} %param.15) | copy-start | bytes 393220
  252.4 52.0 %all-to-all-start.1 = ((bf16[64,128,128]{2,1,0:T(8,128)(2,1)}), bf16[64,128,128]{2,1,0:T(8,128)(2,1)S(1)}, u32[]{:S(2)}, u32[]{:S(2)}) async-start(bf16[64,128,128]{2,1,0:T(8,128)(2,1)} %scatter_fusion), calls=%async_computation.1 | async-start | bytes 4194304 | tf_op jit(solution)/shard_map/all_to_all | solution.py:50
  261.6 588.2 %reduce-scatter.5.cloned.1.call-start = ((), (), s32[]{:S(2)}) async-start(), calls=%async_computation.6 | async-start | bytes 1064960 | tf_op jit(solution)/shard_map/reduce_scatter | solution.py:68
  265.6 3.3 copy-start.3
  268.9 682.5 %reduce-scatter.3.cloned.1.call-start = ((), (), s32[]{:S(2)}) async-start(), calls=%async_computation.5 | async-start | bytes 2359296 | tf_op jit(solution)/shard_map/reduce_scatter | solution.py:63
Sparse Core Ops, SparseCore 0:
  117.5 116.3 all-gather.1
  269.0 580.7 reduce-scatter.4
  852.7 98.7 reduce-scatter.2
where the time goes:
time: 961 us; the launch traced here: 960 us
  waiting for transfers between devices  797 us (83%)
  other arithmetic  57.3 us (6%)
  local copies, waits for them, and re-layouts  47.9 us (5%)
  starting transfers between devices  30.9 us (3%)
  between operations  13.9 us (1%)
  matrix products  12.4 us (1%)
    reduce_scatter x1, waiting for transfers between devices, per_device(): lax.psum_scatter(lax.dot_general(combined, grad_pre, (((0,), (0,)), ((),...  499 us
    all_gather x1, waiting for transfers between devices, per_device(): gathered = lax.all_gather(stacked, 'feat', axis=2, tiled=True)  116 us
    reduce_scatter x1, waiting for transfers between devices, per_device(): lax.psum_scatter(partial_terms, 'feat', scatter_dimension=1, tiled=True)  100 us
    all_to_all x1, waiting for transfers between devices, per_device(): lax.all_to_all(outgoing, 'dom', split_axis=0, concat_axis=0, tiled=True)  47.1 us
    scatter-add x1, other arithmetic, per_device(): neigh_grad.at[target_rows]  44.3 us
    all_to_all x1, waiting for transfers between devices, per_device(): lax.all_to_all(returning, 'dom', split_axis=0, concat_axis=0, tiled=True)  33.9 us
    gather x1, local copies, waits for them, and re-layouts, per_device(): features[safe_rows]  22.8 us
    all_to_all x1, starting transfers between devices, per_device(): lax.all_to_all(outgoing, 'dom', split_axis=0, concat_axis=0, tiled=True)  21.5 us
  transfers between devices with their start and end apart: 5, of which 5 were waited for; matrix products, arithmetic and copies ran while one was open for 6% of the time, Pallas kernels for 0%

commit v1 on v0

--- a/solution.py
+++ b/solution.py
@@ -29,7 +29,9 @@
     aggregate = ((local_sums + remote_sums) / degree_col).astype(jnp.bfloat16)
     stacked = jnp.stack([features, aggregate], axis=1)
     weight_pair = weights.reshape(2, full_width, feat_width)
-    gathered = lax.all_gather(stacked, "feat", axis=2, tiled=True)
+    gathered = jnp.concatenate(
+        lax.all_to_all(jnp.stack([stacked] * lax.axis_size("feat")), "feat", 0, 0), axis=2
+    )
     preact = jnp.einsum("rkc,kcf->rf", gathered, weight_pair, preferred_element_type=jnp.float32)
     output = jax.nn.silu(preact).astype(jnp.bfloat16)
     sigmoid_z = jax.nn.sigmoid(preact)

time: 961 us -> 1010 us (1.051)
  blocking collectives: 0 us -> 154 us
  waiting for transfers between devices: 797 us -> 692 us
    all_to_all x0 -> x1, blocking collectives: none -> 154 us  [per_device(): lax.all_to_all(jnp.stack([stacked] * lax.axis_size('feat')), 'feat', 0, 0)]
    all_gather x1 -> x0, waiting for transfers between devices: 116 us -> none  [per_device(): gathered = lax.all_gather(stacked, 'feat', axis=2, tiled=True)]
    reduce_scatter x1, waiting for transfers between devices: 499 us -> 426 us  [per_device(): lax.psum_scatter(lax.dot_general(combined, grad_pre, (((0,), (0,)), ((),...]
    all_to_all x1, waiting for transfers between devices: 33.9 us -> 95.3 us  [per_device(): lax.all_to_all(returning, 'dom', split_axis=0, concat_axis=0, tiled=True)]
    reduce_scatter x1, waiting for transfers between devices: 100 us -> 124 us  [per_device(): lax.psum_scatter(partial_terms, 'feat', scatter_dimension=1, tiled=True)]
  transfers between devices with their start and end apart: 5 -> 4, of which waited for: 5 -> 4; matrix products, arithmetic and copies ran while one was open for 6% -> 5% of each run, Pallas kernels for 0% -> 0%
where the time goes in v1:
time: 1010 us
  waiting for transfers between devices  692 us (69%)
  blocking collectives  154 us (15%)
  other arithmetic  57 us (6%)
  local copies, waits for them, and re-layouts  53.2 us (5%)
  starting transfers between devices  28.1 us (3%)
  between operations  14.3 us (1%)
    reduce_scatter x1, waiting for transfers between devices, per_device(): lax.psum_scatter(lax.dot_general(combined, grad_pre, (((0,), (0,)), ((),...  426 us
    all_to_all x1, blocking collectives, per_device(): lax.all_to_all(jnp.stack([stacked] * lax.axis_size('feat')), 'feat', 0, 0)  154 us
    reduce_scatter x1, waiting for transfers between devices, per_device(): lax.psum_scatter(partial_terms, 'feat', scatter_dimension=1, tiled=True)  124 us
    all_to_all x1, waiting for transfers between devices, per_device(): lax.all_to_all(returning, 'dom', split_axis=0, concat_axis=0, tiled=True)  95.3 us
    all_to_all x1, waiting for transfers between devices, per_device(): lax.all_to_all(outgoing, 'dom', split_axis=0, concat_axis=0, tiled=True)  47.1 us
    scatter-add x1, other arithmetic, per_device(): neigh_grad.at[target_rows]  44.7 us
    gather x1, local copies, waits for them, and re-layouts, per_device(): features[safe_rows]  22.8 us
    all_to_all x1, starting transfers between devices, per_device(): lax.all_to_all(outgoing, 'dom', split_axis=0, concat_axis=0, tiled=True)  21.5 us
  transfers between devices with their start and end apart: 4, of which 4 were waited for; matrix products, arithmetic and copies ran while one was open for 5% of the time, Pallas kernels for 0%

profile of v1, /device:TPU:8, one launch (start us, length us, event | category | flops | bytes accessed | tf_op | source)
XLA Modules:
  0.0 1008.3 jit_solution(18170420146231371856)
XLA Ops:
  7.2 0.0 copy-start
  7.2 0.8 compare_bitcast_fusion
  8.0 0.8 fusion.10
  8.8 22.8 %gather_fusion = bf16[8192,128]{1,0:T(8,128)(2,1)S(1)} fusion(bf16[512,128]{1,0:T(8,128)(2,1)} %param.8, s32[8192]{0:T(1024)S(1)} %fusion.10), kind=kCustom, calls=%fused_computation | custom fusion | bytes 4227072 | tf_op jit(solution)/shard_map/gather | solution.py:19
  31.6 2.7 broadcast_select_fusion
  34.2 0.0 copy-start.8
  34.2 0.0 copy-start.6
  34.2 21.5 %all-to-all-start = ((bf16[64,128,128]{2,1,0:T(8,128)(2,1)}), bf16[64,128,128]{2,1,0:T(8,128)(2,1)}, u32[]{:S(2)}, u32[]{:S(2)}) async-start(bf16[64,128,128]{2,1,0:T(8,128)(2,1)} %broadcast_select_fusion), calls=%async_computation | async-start | bytes 4194304 | tf_op jit(solution)/shard_map/all_to_all | solution.py:20
  55.8 0.5 broadcast.125
  56.3 0.0 copy-done.8
  56.3 0.7 reduce.3
  56.9 0.1 squeeze.10
  57.0 0.0 copy-done.6
  57.0 0.1 broadcast_bitcast_fusion
  57.1 2.8 reshape.135
  60.0 47.1 %all-to-all-done = bf16[64,128,128]{2,1,0:T(8,128)(2,1)} async-done(((bf16[64,128,128]{2,1,0:T(8,128)(2,1)}), bf16[64,128,128]{2,1,0:T(8,128)(2,1)}, u32[]{:S(2)}, u32[]{:S(2)}) %all-to-all-start) | async-done | bytes 2097184 | tf_op jit(solution)/shard_map/all_to_all | solution.py:20
  107.1 3.7 gather_fusion.1
  110.8 4.4 bitcast_select_fusion
  115.2 0.0 copy-start.1
  115.2 0.0 copy-start.3
  115.2 0.7 fusion.14
  116.0 0.1 copy-done.1
  116.1 0.2 copy-done.3
  116.3 0.3 fusion.5
  116.6 0.1 copy.18
  116.8 0.2 stack.32
  117.0 153.7 %all_to_all.15 = bf16[8,512,2,128]{1,3,2,0:T(8,128)(2,1)} all-to-all(bf16[8,512,2,128]{1,3,2,0:T(8,128)(2,1)S(1)} %stack.32), channel_id=1, replica_groups=mesh['dom'=64,'feat'=8] {'feat'}, dimensions={0} | all-to-all | bytes 4194304 | tf_op jit(solution)/shard_map/all_to_all | solution.py:33
  270.7 4.3 copy.20
  275.0 0.0 copy-start.7
  275.0 4.2 reshape.138
  279.2 0.0 copy-done
  279.2 0.0 copy-done.7
  279.2 3.0 divide_convert_fusion
  282.2 2.1 fusion.2
  284.3 3.0 copy.22
  287.3 1.8 broadcast_in_dim.39
  289.1 8.7 scatter_fusion
  297.8 0.0 copy-start.2
  297.8 6.6 all-to-all-start.2
  304.4 0.0 reduce-scatter.5.cloned.1.call-start
  304.5 0.0 copy-done.2
  304.5 0.2 copy.19
  304.7 0.0 copy-start.5
  304.7 0.0 copy-start.4
  304.7 1.7 fusion.13
  306.4 0.0 reduce-scatter.5.cloned.1.call-update
  306.4 0.0 reduce-scatter.3.cloned.1.call-start
  306.5 0.0 copy-done.5
  306.5 0.1 compare_select_fusion
  306.5 0.0 copy-done.4
  306.5 0.2 convolution_bitcast_fusion.1
  306.8 0.1 copy.23
  306.9 95.3 %all-to-all-done.2 = bf16[64,128,128]{2,1,0:T(8,128)(2,1)} async-done(((bf16[64,128,128]{2,1,0:T(8,128)(2,1)}), bf16[64,128,128]{2,1,0:T(8,128)(2,1)}, u32[]{:S(2)}, u32[]{:S(2)}) %all-to-all-start.2) | async-done | bytes 2097184 | tf_op jit(solution)/shard_map/all_to_all | solution.py:52
  402.2 44.7 %scatter_custom_fusion.1 = f32[512,128]{1,0:T(8,128)S(1)} fusion(f32[512,128]{1,0:T(8,128)S(1)} %copy.23, s32[8192]{0:T(1024)S(1)} %bitcast.80, bf16[8192,128]{1,0:T(8,128)(2,1)} %bitcast.27), kind=kCustom, calls=%fused_computation.4 | custom fusion | flops 2097152 | bytes 2359296 | tf_op jit(solution)/shard_map/scatter-add | solution.py:57
  446.9 1.8 convolution_bitcast_fusion
  448.8 0.0 reduce-scatter.3.cloned.1.call-update
  448.8 425.9 %reduce-scatter.5.cloned.1.call-done = f32[32,128]{1,0:T(8,128)} async-done(((f32[2048,128]{1,0:T(8,128)}), f32[32,128]{1,0:T(8,128)}) %reduce-scatter.5.cloned.1.call-update) | async-done | bytes 16400 | tf_op jit(solution)/shard_map/reduce_scatter | solution.py:70
  874.7 1.3 broadcast_multiply_fusion
  876.0 123.8 %reduce-scatter.3.cloned.1.call-done = f32[512,128]{1,0:T(8,128)} async-done(((f32[512,1024]{1,0:T(8,128)}), f32[512,128]{1,0:T(8,128)}) %reduce-scatter.3.cloned.1.call-update) | async-done | bytes 262160 | tf_op jit(solution)/shard_map/reduce_scatter | solution.py:65
  999.8 1.6 convert_element_type.55
  (7 shorter events, 0.1 us)
Async XLA Ops:
  7.2 272.1 %copy-start = (bf16[2048,128]{1,0:T(8,128)(2,1)S(1)}, bf16[2048,128]{1,0:T(8,128)(2,1)}, u32[]{:S(2)}) copy-start(bf16[2048,128]{1,0:T(8,128)(2,1)} %param.9) | copy-start | bytes 1572868
  34.2 22.0 %copy-start.8 = (s32[1,64]{1,0:T(1,128)S(1)}, s32[1,64]{1,0:T(1,128)}, u32[]{:S(2)}) copy-start(s32[1,64]{1,0:T(1,128)} %param.11) | copy-start | bytes 772
  34.2 22.8 %copy-start.6 = (s32[512]{0:T(512)S(1)}, s32[512]{0:T(512)}, u32[]{:S(2)}) copy-start(s32[512]{0:T(512)} %param.14) | copy-start | bytes 6148
  34.2 72.9 %all-to-all-start = ((bf16[64,128,128]{2,1,0:T(8,128)(2,1)}), bf16[64,128,128]{2,1,0:T(8,128)(2,1)}, u32[]{:S(2)}, u32[]{:S(2)}) async-start(bf16[64,128,128]{2,1,0:T(8,128)(2,1)} %broadcast_select_fusion), calls=%async_computation | async-start | bytes 4194304 | tf_op jit(solution)/shard_map/all_to_all | solution.py:20
  115.2 0.9 copy-start.1
  115.2 1.1 copy-start.3
  275.0 4.2 copy-start.7
  297.8 6.6 copy-start.2
  297.8 104.4 %all-to-all-start.2 = ((bf16[64,128,128]{2,1,0:T(8,128)(2,1)}), bf16[64,128,128]{2,1,0:T(8,128)(2,1)}, u32[]{:S(2)}, u32[]{:S(2)}) async-start(bf16[64,128,128]{2,1,0:T(8,128)(2,1)} %scatter_fusion), calls=%async_computation.2 | async-start | bytes 4194304 | tf_op jit(solution)/shard_map/all_to_all | solution.py:52
  304.4 570.3 %reduce-scatter.5.cloned.1.call-start = ((), (), s32[]{:S(2)}) async-start(), calls=%async_computation.6 | async-start | bytes 1064960 | tf_op jit(solution)/shard_map/reduce_scatter | solution.py:70
  304.7 1.8 copy-start.5
  304.7 1.8 copy-start.4
  306.4 693.4 %reduce-scatter.3.cloned.1.call-start = ((), (), s32[]{:S(2)}) async-start(), calls=%async_computation.5 | async-start | bytes 2359296 | tf_op jit(solution)/shard_map/reduce_scatter | solution.py:65
Sparse Core Ops, SparseCore 0:
  308.0 566.6 reduce-scatter.4
  877.6 122.1 reduce-scatter.2
